TPU v7x, 32 devices: a whole 2x2x4 slice. The times are simulated.
32 devices in a mesh: chol: 8 (over z, x), orb: 4 (over y, core).
Axes of the slice: x: 2, y: 2, z: 4, core: 2. Of those that a mesh axis runs over, the one named last changes fastest.
Arguments:
- b_vectors: bfloat16 [16, 6400, 6400], P('chol', 'orb'), as said below
- gamma_density: bfloat16 [16, 6400, 400], P('chol', 'orb'), may hold values from -2 to 2
Outputs:
- orbital_gradient: float32 [6400, 400], P('orb', 'chol')
Inputs may be any that keep to these rules, and one draw needn't show every extreme that they name: Each b_vectors[Q] is a symmetric matrix.
All inputs are finite; a program needn't handle non-finite values.
Results may differ from a plain program's by a relative error of at most 0.0003.
Values may be sent and summed in bfloat16 or wider, within the bound.
A program may use at most 128 MiB of HBM per device.

v0:
```python
import functools

import jax
import jax.numpy as jnp
from jax import lax
from jax.experimental import pallas as pl
from jax.experimental.pallas import tpu as pltpu
from jax.sharding import PartitionSpec as P

LANES = 128
PAIR = 2
LAG1, LAG2, LAG3, HOP = 1, 3, 5, 2
MESH = pl.DeviceIdType.MESH
F32 = jnp.float32


def gathered(b_vectors, gamma_density):
    partial_sum = jnp.einsum(
        "qpr,qri->pi",
        b_vectors,
        lax.all_gather(gamma_density, "orb", axis=1, tiled=True),
        preferred_element_type=F32,
    )
    row_block = lax.psum_scatter(partial_sum, "chol", scatter_dimension=1, tiled=True)
    stride = b_vectors.shape[2] // gamma_density.shape[2]
    own_occupied = row_block[::stride]
    full_columns = lax.all_gather(own_occupied, "chol", axis=1, tiled=True)
    exchanged = lax.all_to_all(full_columns, "orb", split_axis=1, concat_axis=0, tiled=True)
    flipped = exchanged.T
    col_offset = lax.axis_index("chol") * row_block.shape[1]
    mirrored = lax.dynamic_slice_in_dim(flipped, col_offset, row_block.shape[1], 1)
    return row_block.at[::stride].set(own_occupied - mirrored)


def kernel(nz, rows, cols, stride, ha,
           b_ref, g_ref, out_ref,
           bbuf, gt, cbuf, rc, s, rx1, ry1, rx2, ry2, zown, zr, zl, f, ms, mr,
           bsem, csem, x1sem, y1sem, x2sem, y2sem, rsem, lsem, msem):
    c, o = lax.axis_index("chol"), lax.axis_index("orb")
    z, x = c // PAIR, lax.rem(c, PAIR)
    y, k = o // PAIR, lax.rem(o, PAIR)
    nvec = b_ref.shape[0]
    nocc = g_ref.shape[1]
    hx = nocc // PAIR
    half = PAIR * rows
    nch = s.shape[0]
    shift = half // LANES - nch
    zrows = zown.shape[2]

    core_id = (c, o + 1 - 2 * k)
    x_id = (c + 1 - 2 * x, o)
    y_id = (c, o + PAIR - 2 * PAIR * y)
    right_id = (c + PAIR, o)
    left_id = (c - PAIR, o)

    def fetches(j, side):
        quadrant = 1 - k if side == 0 else k
        slot = PAIR * lax.rem(j, 2) + side
        out = []
        for q in range(nvec):
            for yy in range(PAIR):
                lane = pl.multiple_of((yy * (half // LANES) + quadrant * shift + j) * LANES, LANES)
                out.append(pltpu.make_async_copy(
                    b_ref.at[q, :, pl.ds(lane, LANES)],
                    bbuf.at[slot, q * rows:(q + 1) * rows, yy * LANES:(yy + 1) * LANES],
                    bsem.at[slot, q * PAIR + yy]))
        return out

    def remote(src, dst, sems, j, target):
        return pltpu.make_async_remote_copy(
            src_ref=src, dst_ref=dst, send_sem=sems.at[0, j], recv_sem=sems.at[1, j],
            device_id=target, device_id_type=MESH)

    def core_copy(j):
        return remote(cbuf.at[j], rc.at[j], csem, j, core_id)

    def x1_copy(j):
        return remote(s.at[j, :, 1 - x, 0:ha], rx1.at[j], x1sem, j, x_id)

    def y1_copy(j):
        return remote(s.at[j, 1 - y, :, ha:hx], ry1.at[j], y1sem, j, y_id)

    def y2_copy(j):
        return remote(s.at[j, 1 - y, x, 0:ha], ry2.at[j], y2sem, j, y_id)

    def x2_copy(j):
        return remote(s.at[j, y, 1 - x, ha:hx], rx2.at[j], x2sem, j, x_id)

    def right_copy(j, first):
        return remote(zown.at[j, first:nz], zr.at[j, first:nz], rsem, j, right_id)

    def left_copy(j, last):
        return remote(zown.at[j, 0:last], zl.at[j, 0:last], lsem, j, left_id)

    for j in range(2):
        for side in range(2):
            for copy in fetches(j, side):
                copy.start()

    barrier = pltpu.get_barrier_semaphore()

    def greet(target):
        pl.semaphore_signal(barrier, inc=1, device_id=target, device_id_type=MESH)

    for target in (core_id, x_id, y_id):
        greet(target)

    @pl.when(z > 0)
    def _():
        greet(left_id)

    @pl.when(z < nz - 1)
    def _():
        greet(right_id)

    for h in range(2):
        @pl.when(2 * o + h != c)
        def _():
            greet((2 * o + h, c // 2))

    col = lax.broadcasted_iota(jnp.int32, (nocc, nocc), 1)
    row = lax.broadcasted_iota(jnp.int32, (nocc, nocc), 0)
    origin = row
    for xx in range(PAIR):
        for zz in range(nz):
            start = xx * hx + zz * cols
            delta = (zz * PAIR + xx) * cols - start
            origin = jnp.where((row >= start) & (row < start + cols), row + delta, origin)
    pick = jnp.where(col == origin, 1.0, 0.0).astype(jnp.bfloat16)
    parts = [jnp.dot(pick, g_ref[q], preferred_element_type=F32) for q in range(nvec)]
    gt[...] = jnp.concatenate(parts, axis=1).astype(jnp.bfloat16)

    count = 3 + jnp.where(z > 0, 1, 0) + jnp.where(z < nz - 1, 1, 0) + jnp.where(c // 2 == o, 1, 2)
    pl.semaphore_wait(barrier, count)

    def product(t, side):
        slot = PAIR * lax.rem(t, 2) + side
        for copy in fetches(t, side):
            copy.wait()
        dst = cbuf if side == 0 else s
        res = jnp.dot(gt[...], bbuf[slot], preferred_element_type=F32)
        for yy in range(PAIR):
            for xx in range(PAIR):
                dst[t, yy, xx] = res[xx * hx:(xx + 1) * hx, yy * LANES:(yy + 1) * LANES]

        @pl.when(t + 2 < nch)
        def _():
            for copy in fetches(t + 2, side):
                copy.start()

    def at_lag(t, lag, run):
        j = t - lag

        @pl.when((j >= 0) & (j < nch))
        def _():
            run(j)

    def between_cores(j):
        core_copy(j).wait_recv()
        s[j] = s[j] + rc[j]
        x1_copy(j).start()
        y1_copy(j).start()

    def first_done(j):
        x1_copy(j).wait_recv()
        for yy in range(PAIR):
            s[j, yy, x, 0:ha] = s[j, yy, x, 0:ha] + rx1[j, yy]
        y2_copy(j).start()
        y1_copy(j).wait_recv()
        for xx in range(PAIR):
            s[j, y, xx, ha:hx] = s[j, y, xx, ha:hx] + ry1[j, xx]
        x2_copy(j).start()

    def second_done(j):
        y2_copy(j).wait_recv()
        x2_copy(j).wait_recv()
        top = s[j, y, x, 0:ha] + ry2[j]
        bottom = s[j, y, x, ha:hx] + rx2[j]
        whole = jnp.concatenate([top, bottom, jnp.zeros((8, LANES), F32)], axis=0)
        for zz in range(nz):
            zown[j, zz] = whole[zz * cols:zz * cols + zrows]

    def hop(h, j):
        @pl.when(z == h)
        def _():
            if h > 0:
                right_copy(j, h).wait_recv()
                for d in range(h + 1, nz):
                    zown[j, d] = zown[j, d] + zr[j, d]
            if h < nz - 1:
                right_copy(j, h + 1).start()

        m = nz - 1 - h

        @pl.when(z == m)
        def _():
            if h > 0:
                left_copy(j, m + 1).wait_recv()
                for d in range(m):
                    zown[j, d] = zown[j, d] + zl[j, d]
            if m > 0:
                left_copy(j, m).start()

    def collect(j):
        for h in range(nz):
            @pl.when(z == h)
            def _():
                total = zown[j, h]
                if h > 0:
                    total = total + zr[j, h]
                if h < nz - 1:
                    total = total + zl[j, h]
                square = jnp.concatenate([total, jnp.zeros((LANES - zrows, LANES), F32)], axis=0)
                f[pl.ds(pl.multiple_of(j * LANES, LANES), LANES), :] = square.T

    def step(t, carry):
        @pl.when(t < nch)
        def _():
            product(t, 0)
            core_copy(t).start()

        at_lag(t, LAG1, between_cores)
        at_lag(t, LAG2, first_done)
        at_lag(t, LAG3, second_done)
        for h in range(nz):
            at_lag(t, LAG3 + HOP * h, functools.partial(hop, h))
        at_lag(t, LAG3 + HOP * (nz - 1), collect)

        @pl.when(t < nch)
        def _():
            product(t, 1)

        return carry

    lax.fori_loop(0, nch + LAG3 + HOP * (nz - 1), step, 0)

    off = k * (rows - shift * LANES)

    def mirror_copy(h, slot):
        return pltpu.make_async_remote_copy(
            src_ref=ms.at[h], dst_ref=mr.at[slot], send_sem=msem.at[0, h], recv_sem=msem.at[1, slot],
            device_id=(2 * o + h, c // 2), device_id_type=MESH)

    for h in range(2):
        block = f[pl.ds(off + h * stride * cols, cols, stride), :]
        ms[h] = jnp.concatenate([block, jnp.zeros((zrows - cols, LANES), F32)], axis=0)

        @pl.when(2 * o + h != c)
        def _():
            mirror_copy(h, x).start()

        @pl.when(2 * o + h == c)
        def _():
            mr[x] = ms[h]

    def drain(j, carry):
        for copy in (core_copy, x1_copy, y1_copy, x2_copy, y2_copy):
            copy(j).wait_send()
        for h in range(nz):
            @pl.when(z == h)
            def _():
                if h < nz - 1:
                    right_copy(j, h + 1).wait_send()
                if h > 0:
                    left_copy(j, h).wait_send()
        return carry

    lax.fori_loop(0, nch, drain, 0)

    for h in range(2):
        @pl.when(2 * o + h != c)
        def _():
            mirror_copy(h, x).wait_send()
            mirror_copy(h, h).wait_recv()

    for h in range(2):
        square = jnp.concatenate([mr[h], jnp.zeros((LANES - zrows, LANES), F32)], axis=0).T
        where = pl.ds(off + h * stride * cols, cols, stride)
        f[where, :] = f[where, :] - square[0:cols]
    out_ref[...] = f[pl.ds(pl.multiple_of(off, 8), rows), 0:cols]


def mirrored_sums(nz, b_vectors, gamma_density):
    nvec, rows, nmo = b_vectors.shape
    nocc = gamma_density.shape[2]
    cols = nocc // (nz * PAIR)
    hx = nocc // PAIR
    ha = (hx // 2 + 7) // 8 * 8
    zrows = (cols + 7) // 8 * 8
    nch = pl.cdiv(rows, LANES)
    depth = nvec * rows
    vmem = pltpu.VMEM
    dma = pltpu.SemaphoreType.DMA
    flops = 2 * depth * nmo * nocc
    return pl.pallas_call(
        functools.partial(kernel, nz, rows, cols, nmo // nocc, ha),
        out_shape=jax.ShapeDtypeStruct((rows, cols), F32),
        in_specs=[pl.BlockSpec(memory_space=pl.ANY), pl.BlockSpec(memory_space=vmem)],
        out_specs=pl.BlockSpec(memory_space=vmem),
        scratch_shapes=[
            vmem((2 * PAIR, depth, PAIR * LANES), jnp.bfloat16),
            vmem((nocc, depth), jnp.bfloat16),
            vmem((nch, PAIR, PAIR, hx, LANES), F32),
            vmem((nch, PAIR, PAIR, hx, LANES), F32),
            vmem((nch, PAIR, PAIR, hx, LANES), F32),
            vmem((nch, PAIR, ha, LANES), F32),
            vmem((nch, PAIR, hx - ha, LANES), F32),
            vmem((nch, hx - ha, LANES), F32),
            vmem((nch, ha, LANES), F32),
            vmem((nch, nz, zrows, LANES), F32),
            vmem((nch, nz, zrows, LANES), F32),
            vmem((nch, nz, zrows, LANES), F32),
            vmem((nch * LANES, LANES), F32),
            vmem((2, zrows, LANES), F32),
            vmem((2, zrows, LANES), F32),
            dma((2 * PAIR, nvec * PAIR)),
            dma((2, nch)),
            dma((2, nch)),
            dma((2, nch)),
            dma((2, nch)),
            dma((2, nch)),
            dma((2, nch)),
            dma((2, nch)),
            dma((2, 2)),
        ],
        compiler_params=pltpu.CompilerParams(
            collective_id=0, has_side_effects=True, vmem_limit_bytes=60 * 2**20
        ),
        cost_estimate=pl.CostEstimate(flops=flops, bytes_accessed=2 * depth * nmo, transcendentals=0),
    )(b_vectors, jnp.transpose(gamma_density, (0, 2, 1)))


def solution(mesh):
    nchol, norb = mesh.shape["chol"], mesh.shape["orb"]

    def shards(b_vectors, gamma_density):
        nvec, rows, nmo = b_vectors.shape
        nocc = gamma_density.shape[2]
        fits = (
            norb == PAIR * PAIR
            and nchol == PAIR * norb
            and (PAIR * rows) % LANES == 0
            and rows % 16 == 0
            and nocc % (PAIR * nchol) == 0
            and (nocc // PAIR) % 8 == 0
            and (nvec * rows) % LANES == 0
            and nmo % nocc == 0
            and rows % (nmo // nocc) == 0
        )
        if fits:
            return mirrored_sums(nchol // PAIR, b_vectors, gamma_density)
        return gathered(b_vectors, gamma_density)

    in_specs = (P("chol", "orb", None), P("chol", "orb", None))
    out_specs = P("orb", "chol")
    return jax.shard_map(shards, mesh=mesh, in_specs=in_specs, out_specs=out_specs, check_vma=False)
```

profile of v0, /device:TPU:0, one launch (start us, length us, event | category | flops | bytes accessed | tf_op | source)
XLA Modules:
  0.0 73.8 jit_solution(15008430320115674936)
XLA Ops:
  0.0 71.6 %shard_map.28 = f32[1600,50]{1,0:T(8,128)} custom-call(bf16[2,1600,6400]{2,1,0:T(8,128)(2,1)} %b_ref.1, bf16[2,400,1600]{2,1,0:T(8,128)(2,1)} %bitcast.1), custom_call_target="tpu_custom_call" | custom-call | flops 16384000000 | bytes 40960000 | tf_op jit(solution)/shard_map/pallas_call | solution.py:295
  71.6 2.2 %copy.3 = f32[1600,50]{0,1:T(8,128)} copy(f32[1600,50]{1,0:T(8,128)} %shard_map.28) | data formatting | bytes 640000 | tf_op jit(solution)/shard_map/pallas_call | solution.py:295
where the time goes:
time: 74.1 us; the launch traced here: 73.8 us
  Pallas kernels  71.6 us (97%)
  local copies, waits for them, and re-layouts  2.19 us (3%)
    pallas_call x1, Pallas kernels, mirrored_sums(): pl.pallas_call(functools.partial(kernel, nz, rows, cols, nmo // nocc, ha)...  71.6 us
    pallas_call x1, local copies, waits for them, and re-layouts, mirrored_sums(): pl.pallas_call(functools.partial(kernel, nz, rows, cols, nmo // nocc, ha)...  2.19 us

commit v1 on v0

v1 whole, which is shorter than its diff:
```python
import functools

import jax
import jax.numpy as jnp
from jax import lax
from jax.experimental import pallas as pl
from jax.experimental.pallas import tpu as pltpu
from jax.sharding import PartitionSpec as P

LANES = 128
PAIR = 2
SUB = 8
LAGS = 1, 3, 5, 7, 9
MESH = pl.DeviceIdType.MESH
F32 = jnp.float32


def gathered(b_vectors, gamma_density):
    partial_sum = jnp.einsum(
        "qpr,qri->pi",
        b_vectors,
        lax.all_gather(gamma_density, "orb", axis=1, tiled=True),
        preferred_element_type=F32,
    )
    row_block = lax.psum_scatter(partial_sum, "chol", scatter_dimension=1, tiled=True)
    stride = b_vectors.shape[2] // gamma_density.shape[2]
    own_occupied = row_block[::stride]
    full_columns = lax.all_gather(own_occupied, "chol", axis=1, tiled=True)
    exchanged = lax.all_to_all(full_columns, "orb", split_axis=1, concat_axis=0, tiled=True)
    flipped = exchanged.T
    col_offset = lax.axis_index("chol") * row_block.shape[1]
    mirrored = lax.dynamic_slice_in_dim(flipped, col_offset, row_block.shape[1], 1)
    return row_block.at[::stride].set(own_occupied - mirrored)


FINE, COARSE, SPLIT, BASE = 65535.0, 32385.0, 256.0, 255.0


def packed_tiles(n):
    return n - n // 3 + 1


def packed(v):
    m = v.shape[0] // 3
    top = jnp.maximum(jnp.max(jnp.abs(v), axis=0), 1e-30)
    fine = FINE / top
    coarse = COARSE / top
    a = jnp.round(v[0:m] * fine)
    b = jnp.round(v[m:2 * m] * fine)
    c = jnp.round(v[2 * m:3 * m] * coarse)
    high = jnp.round(c * (1 / BASE))
    low = c - high * BASE
    rest = [v[3 * m:]] if v.shape[0] > 3 * m else []
    return jnp.concatenate([a * SPLIT + high, b * SPLIT + low, *rest, top[None]], axis=0)


def opened(w, rest):
    m = (w.shape[0] - 1 - rest) // 2
    top = w[2 * m + rest]
    fine = top * (1 / FINE)
    coarse = top * (1 / COARSE)
    first, second = w[0:m], w[m:2 * m]
    a = jnp.round(first * (1 / SPLIT))
    b = jnp.round(second * (1 / SPLIT))
    c = (first - a * SPLIT) * BASE + (second - b * SPLIT)
    tail = [w[2 * m:2 * m + rest]] if rest else []
    return jnp.concatenate([a * fine, b * fine, c * coarse, *tail], axis=0)


def kernel(nz, rows, cols, stride, ta,
           b_ref, g_ref, out_ref,
           bbuf, gt, cbuf, rc, s, ex1, ey1, ex2, ey2, rx1, ry1, rx2, ry2, own, z1r, z2s, z2r, f, ms, mr,
           bsem, csem, x1sem, y1sem, x2sem, y2sem, z1sem, z2sem, msem):
    c, o = lax.axis_index("chol"), lax.axis_index("orb")
    z, x = c // PAIR, lax.rem(c, PAIR)
    y, k = o // PAIR, lax.rem(o, PAIR)
    zl, zh = lax.rem(z, 2), z // 2
    nvec = b_ref.shape[0]
    nocc = g_ref.shape[1]
    hx = nocc // PAIR
    tiles = hx // SUB
    tb = tiles - ta
    half = PAIR * rows
    nch = s.shape[0]
    shift = half // LANES - nch
    tz = z1r.shape[2]
    zstep = cols // SUB
    zrows = tz * SUB

    core_id = (c, o + 1 - 2 * k)
    x_id = (c + 1 - 2 * x, o)
    y_id = (c, o + PAIR - 2 * PAIR * y)
    near_id = (c + PAIR - 2 * PAIR * zl, o)
    far_id = (c + 2 * PAIR - 4 * PAIR * zh, o)

    def fetches(j, side):
        quadrant = 1 - k if side == 0 else k
        slot = PAIR * lax.rem(j, 2) + side
        out = []
        for q in range(nvec):
            for yy in range(PAIR):
                lane = pl.multiple_of((yy * (half // LANES) + quadrant * shift + j) * LANES, LANES)
                out.append(pltpu.make_async_copy(
                    b_ref.at[q, :, pl.ds(lane, LANES)],
                    bbuf.at[slot, q * rows:(q + 1) * rows, yy * LANES:(yy + 1) * LANES],
                    bsem.at[slot, q * PAIR + yy]))
        return out

    def remote(src, dst, send, recv, target):
        return pltpu.make_async_remote_copy(
            src_ref=src, dst_ref=dst, send_sem=send, recv_sem=recv,
            device_id=target, device_id_type=MESH)

    def core_copy(j):
        return remote(cbuf.at[j], rc.at[j], csem.at[0, j], csem.at[1, j], core_id)

    def x1_copy(j):
        return remote(ex1.at[j], rx1.at[j], x1sem.at[0, j], x1sem.at[1, j], x_id)

    def y1_copy(j):
        return remote(ey1.at[j], ry1.at[j], y1sem.at[0, j], y1sem.at[1, j], y_id)

    def y2_copy(j):
        return remote(ey2.at[j], ry2.at[j], y2sem.at[0, j], y2sem.at[1, j], y_id)

    def x2_copy(j):
        return remote(ex2.at[j], rx2.at[j], x2sem.at[0, j], x2sem.at[1, j], x_id)

    def near_copy(j, h):
        first = (1 - zl + 2 * h) * zstep
        return remote(own.at[j, pl.ds(first, tz)], z1r.at[j, h], z1sem.at[0, j, h], z1sem.at[1, j, h], near_id)

    def far_copy(j):
        return remote(z2s.at[j, 1 - zh], z2r.at[j], z2sem.at[0, j], z2sem.at[1, j], far_id)

    for j in range(2):
        for side in range(2):
            for copy in fetches(j, side):
                copy.start()

    barrier = pltpu.get_barrier_semaphore()

    def greet(target):
        pl.semaphore_signal(barrier, inc=1, device_id=target, device_id_type=MESH)

    for target in (core_id, x_id, y_id, near_id, far_id):
        greet(target)

    for h in range(2):
        @pl.when(2 * o + h != c)
        def _():
            greet((2 * o + h, c // 2))

    col = lax.broadcasted_iota(jnp.int32, (nocc, nocc), 1)
    row = lax.broadcasted_iota(jnp.int32, (nocc, nocc), 0)
    origin = row
    for xx in range(PAIR):
        for zz in range(nz):
            start = xx * hx + zz * cols
            delta = (zz * PAIR + xx) * cols - start
            origin = jnp.where((row >= start) & (row < start + cols), row + delta, origin)
    pick = jnp.where(col == origin, 1.0, 0.0).astype(jnp.bfloat16)
    parts = [jnp.dot(pick, g_ref[q], preferred_element_type=F32) for q in range(nvec)]
    gt[...] = jnp.concatenate(parts, axis=1).astype(jnp.bfloat16)

    count = 5 + jnp.where(c // 2 == o, 1, 2)
    pl.semaphore_wait(barrier, count)

    def product(t, side):
        slot = PAIR * lax.rem(t, 2) + side
        for copy in fetches(t, side):
            copy.wait()
        dst = cbuf if side == 0 else s
        res = jnp.dot(gt[...], bbuf[slot], preferred_element_type=F32)
        for yy in range(PAIR):
            for xx in range(PAIR):
                part = res[xx * hx:(xx + 1) * hx, yy * LANES:(yy + 1) * LANES]
                dst[t, yy, xx] = part.reshape(tiles, SUB, LANES)

        @pl.when(t + 2 < nch)
        def _():
            for copy in fetches(t + 2, side):
                copy.start()

    def at_lag(t, lag, run):
        j = t - lag

        @pl.when((j >= 0) & (j < nch))
        def _():
            run(j)

    def between_cores(j):
        core_copy(j).wait_recv()
        away = [s[j, yy, 1 - x, 0:ta] + rc[j, yy, 1 - x, 0:ta] for yy in range(PAIR)]
        ex1[j] = packed(jnp.concatenate(away, axis=0))
        x1_copy(j).start()
        away = [s[j, 1 - y, xx, ta:tiles] + rc[j, 1 - y, xx, ta:tiles] for xx in range(PAIR)]
        ey1[j] = packed(jnp.concatenate(away, axis=0))
        y1_copy(j).start()
        for yy in range(PAIR):
            s[j, yy, x, 0:ta] = s[j, yy, x, 0:ta] + rc[j, yy, x, 0:ta]
        for xx in range(PAIR):
            s[j, y, xx, ta:tiles] = s[j, y, xx, ta:tiles] + rc[j, y, xx, ta:tiles]

    def first_done(j):
        x1_copy(j).wait_recv()
        arrived = opened(rx1[j], PAIR * ta % 3)
        s[j, 0, x, 0:ta] = s[j, 0, x, 0:ta] + arrived[0:ta]
        s[j, 1, x, 0:ta] = s[j, 1, x, 0:ta] + arrived[ta:2 * ta]
        ey2[j] = packed(s[j, 1 - y, x, 0:ta])
        y2_copy(j).start()
        y1_copy(j).wait_recv()
        arrived = opened(ry1[j], PAIR * tb % 3)
        s[j, y, 0, ta:tiles] = s[j, y, 0, ta:tiles] + arrived[0:tb]
        s[j, y, 1, ta:tiles] = s[j, y, 1, ta:tiles] + arrived[tb:2 * tb]
        ex2[j] = packed(s[j, y, 1 - x, ta:tiles])
        x2_copy(j).start()

    def second_done(j):
        y2_copy(j).wait_recv()
        own[j, 0:ta] = s[j, y, x, 0:ta] + opened(ry2[j], ta % 3)
        x2_copy(j).wait_recv()
        own[j, ta:tiles] = s[j, y, x, ta:tiles] + opened(rx2[j], tb % 3)
        for h in range(2):
            near_copy(j, h).start()

    def near_done(j):
        for h in range(2):
            near_copy(j, h).wait_recv()
            z2s[j, h] = own[j, pl.ds((zl + 2 * h) * zstep, tz)] + z1r[j, h]
        far_copy(j).start()

    def collect(j):
        far_copy(j).wait_recv()
        total = (z2s[j, zh] + z2r[j]).reshape(zrows, LANES)
        for h in range(nz):
            @pl.when(z == h)
            def _():
                lead = h * (cols - zstep * SUB)
                square = jnp.concatenate([total[lead:lead + cols], jnp.zeros((LANES - cols, LANES), F32)], axis=0)
                f[pl.ds(pl.multiple_of(j * LANES, LANES), LANES), :] = square.T

    def step(t, carry):
        @pl.when(t < nch)
        def _():
            product(t, 0)
            core_copy(t).start()

        at_lag(t, LAGS[0], between_cores)
        at_lag(t, LAGS[1], first_done)
        at_lag(t, LAGS[2], second_done)
        at_lag(t, LAGS[3], near_done)
        at_lag(t, LAGS[4], collect)

        @pl.when(t < nch)
        def _():
            product(t, 1)

        return carry

    lax.fori_loop(0, nch + LAGS[4], step, 0)

    off = k * (rows - shift * LANES)

    def mirror_copy(h, slot):
        return remote(ms.at[h], mr.at[slot], msem.at[0, h], msem.at[1, slot], (2 * o + h, c // 2))

    for h in range(2):
        block = f[pl.ds(off + h * stride * cols, cols, stride), :]
        ms[h] = jnp.concatenate([block, jnp.zeros((zrows - cols, LANES), F32)], axis=0)

        @pl.when(2 * o + h != c)
        def _():
            mirror_copy(h, x).start()

        @pl.when(2 * o + h == c)
        def _():
            mr[x] = ms[h]

    def drain(j, carry):
        for copy in (core_copy, x1_copy, y1_copy, x2_copy, y2_copy, far_copy):
            copy(j).wait_send()
        for h in range(2):
            near_copy(j, h).wait_send()
        return carry

    lax.fori_loop(0, nch, drain, 0)

    for h in range(2):
        @pl.when(2 * o + h != c)
        def _():
            mirror_copy(h, x).wait_send()
            mirror_copy(h, h).wait_recv()

    for h in range(2):
        square = jnp.concatenate([mr[h], jnp.zeros((LANES - zrows, LANES), F32)], axis=0).T
        where = pl.ds(off + h * stride * cols, cols, stride)
        f[where, :] = f[where, :] - square[0:cols]
    out_ref[...] = f[pl.ds(pl.multiple_of(off, 8), rows), 0:cols]


def mirrored_sums(nz, b_vectors, gamma_density):
    nvec, rows, nmo = b_vectors.shape
    nocc = gamma_density.shape[2]
    cols = nocc // (nz * PAIR)
    hx = nocc // PAIR
    tiles = hx // SUB
    ta = (tiles + 1) // 2
    tb = tiles - ta
    tz = pl.cdiv(cols, SUB)
    nch = pl.cdiv(rows, LANES)
    depth = nvec * rows
    vmem = pltpu.VMEM
    dma = pltpu.SemaphoreType.DMA
    flops = 2 * depth * nmo * nocc
    parts = [packed_tiles(n) for n in (PAIR * ta, PAIR * tb, tb, ta)]
    blocks = [vmem((nch, n, SUB, LANES), F32) for n in parts]
    return pl.pallas_call(
        functools.partial(kernel, nz, rows, cols, nmo // nocc, ta),
        out_shape=jax.ShapeDtypeStruct((rows, cols), F32),
        in_specs=[pl.BlockSpec(memory_space=pl.ANY), pl.BlockSpec(memory_space=vmem)],
        out_specs=pl.BlockSpec(memory_space=vmem),
        scratch_shapes=[
            vmem((2 * PAIR, depth, PAIR * LANES), jnp.bfloat16),
            vmem((nocc, depth), jnp.bfloat16),
            vmem((nch, PAIR, PAIR, tiles, SUB, LANES), F32),
            vmem((nch, PAIR, PAIR, tiles, SUB, LANES), F32),
            vmem((nch, PAIR, PAIR, tiles, SUB, LANES), F32),
            *blocks,
            *blocks,
            vmem((nch, tiles, SUB, LANES), F32),
            vmem((nch, 2, tz, SUB, LANES), F32),
            vmem((nch, 2, tz, SUB, LANES), F32),
            vmem((nch, tz, SUB, LANES), F32),
            vmem((nch * LANES, LANES), F32),
            vmem((2, tz * SUB, LANES), F32),
            vmem((2, tz * SUB, LANES), F32),
            dma((2 * PAIR, nvec * PAIR)),
            dma((2, nch)),
            dma((2, nch)),
            dma((2, nch)),
            dma((2, nch)),
            dma((2, nch)),
            dma((2, nch, 2)),
            dma((2, nch)),
            dma((2, 2)),
        ],
        compiler_params=pltpu.CompilerParams(
            collective_id=0, has_side_effects=True, vmem_limit_bytes=60 * 2**20
        ),
        cost_estimate=pl.CostEstimate(flops=flops, bytes_accessed=2 * depth * nmo, transcendentals=0),
    )(b_vectors, jnp.transpose(gamma_density, (0, 2, 1)))


def solution(mesh):
    nchol, norb = mesh.shape["chol"], mesh.shape["orb"]

    def shards(b_vectors, gamma_density):
        nvec, rows, nmo = b_vectors.shape
        nocc = gamma_density.shape[2]
        cols = nocc // nchol
        fits = (
            norb == PAIR * PAIR
            and nchol == PAIR * norb
            and (PAIR * rows) % LANES == 0
            and rows % 16 == 0
            and nocc % (PAIR * nchol) == 0
            and (nocc // PAIR) % SUB == 0
            and nchol == 8
            and cols % SUB * (nchol // PAIR) <= SUB
            and (nvec * rows) % LANES == 0
            and nmo % nocc == 0
            and rows % (nmo // nocc) == 0
        )
        if fits:
            return mirrored_sums(nchol // PAIR, b_vectors, gamma_density)
        return gathered(b_vectors, gamma_density)

    in_specs = (P("chol", "orb", None), P("chol", "orb", None))
    out_specs = P("orb", "chol")
    return jax.shard_map(shards, mesh=mesh, in_specs=in_specs, out_specs=out_specs, check_vma=False)
```

time: 74.1 us -> 61.5 us (0.83)
  Pallas kernels: 71.6 us -> 58.7 us
    pallas_call x1, Pallas kernels: 71.6 us -> 58.7 us  [mirrored_sums(): pl.pallas_call(functools.partial(kernel, nz, rows, cols, nmo // nocc, ta)...]
where the time goes in v1:
time: 61.5 us; the launch traced here: 60.9 us
  Pallas kernels  58.7 us (95%)
  local copies, waits for them, and re-layouts  2.19 us (4%)
    pallas_call x1, Pallas kernels, mirrored_sums(): pl.pallas_call(functools.partial(kernel, nz, rows, cols, nmo // nocc, ta)...  58.7 us
    pallas_call x1, local copies, waits for them, and re-layouts, mirrored_sums(): pl.pallas_call(functools.partial(kernel, nz, rows, cols, nmo // nocc, ta)...  2.19 us

profile of v1, /device:TPU:0, one launch (start us, length us, event | category | flops | bytes accessed | tf_op | source)
XLA Modules:
  0.0 60.9 jit_solution(7350842591950928419)
XLA Ops:
  0.0 58.7 %shard_map.28 = f32[1600,50]{1,0:T(8,128)} custom-call(bf16[2,1600,6400]{2,1,0:T(8,128)(2,1)} %b_ref.1, bf16[2,400,1600]{2,1,0:T(8,128)(2,1)} %bitcast.1), custom_call_target="tpu_custom_call" | custom-call | flops 16384000000 | bytes 40960000 | tf_op jit(solution)/shard_map/pallas_call | solution.py:318
  58.7 2.2 %copy.3 = f32[1600,50]{0,1:T(8,128)} copy(f32[1600,50]{1,0:T(8,128)} %shard_map.28) | data formatting | bytes 640000 | tf_op jit(solution)/shard_map/pallas_call | solution.py:318

commit v2 on v1

--- a/solution.py
+++ b/solution.py
@@ -10,7 +10,7 @@
 LANES = 128
 PAIR = 2
 SUB = 8
-LAGS = 1, 3, 5, 7, 9
+LAGS = 1, 4, 7, 10, 13
 MESH = pl.DeviceIdType.MESH
 F32 = jnp.float32
 
@@ -34,43 +34,72 @@
 
 
 FINE, COARSE, SPLIT, BASE = 65535.0, 32385.0, 256.0, 255.0
+EVEN, SLOT, STEP, NINE = 8187.0, 2048.0, 8.0, 9.0
+
+
+def grouping(n):
+    sevens, left = divmod(n, 7)
+    threes, rest = divmod(left, 3)
+    return sevens, threes, rest
 
 
 def packed_tiles(n):
-    return n - n // 3 + 1
+    sevens, threes, rest = grouping(n)
+    return 4 * sevens + 2 * threes + rest + 1
 
 
 def packed(v):
-    m = v.shape[0] // 3
+    m, t, rest = grouping(v.shape[0])
     top = jnp.maximum(jnp.max(jnp.abs(v), axis=0), 1e-30)
-    fine = FINE / top
-    coarse = COARSE / top
-    a = jnp.round(v[0:m] * fine)
-    b = jnp.round(v[m:2 * m] * fine)
-    c = jnp.round(v[2 * m:3 * m] * coarse)
-    high = jnp.round(c * (1 / BASE))
-    low = c - high * BASE
-    rest = [v[3 * m:]] if v.shape[0] > 3 * m else []
-    return jnp.concatenate([a * SPLIT + high, b * SPLIT + low, *rest, top[None]], axis=0)
-
-
-def opened(w, rest):
-    m = (w.shape[0] - 1 - rest) // 2
-    top = w[2 * m + rest]
-    fine = top * (1 / FINE)
-    coarse = top * (1 / COARSE)
-    first, second = w[0:m], w[m:2 * m]
-    a = jnp.round(first * (1 / SPLIT))
-    b = jnp.round(second * (1 / SPLIT))
-    c = (first - a * SPLIT) * BASE + (second - b * SPLIT)
-    tail = [w[2 * m:2 * m + rest]] if rest else []
-    return jnp.concatenate([a * fine, b * fine, c * coarse, *tail], axis=0)
+    words = []
+    if m:
+        even = EVEN / top
+        q = [jnp.round(v[i * m:(i + 1) * m] * even) for i in range(7)]
+        high = [jnp.round(e * (1 / STEP)) for e in q[4:]]
+        low = [e - h * STEP for e, h in zip(q[4:], high)]
+        high.append((low[0] * NINE + low[1]) * NINE + low[2])
+        words += [a * SLOT + h for a, h in zip(q[:4], high)]
+    if t:
+        u = v[7 * m:7 * m + 3 * t]
+        fine, coarse = FINE / top, COARSE / top
+        a, b, c = jnp.round(u[0:t] * fine), jnp.round(u[t:2 * t] * fine), jnp.round(u[2 * t:3 * t] * coarse)
+        high = jnp.round(c * (1 / BASE))
+        words += [a * SPLIT + high, b * SPLIT + (c - high * BASE)]
+    if rest:
+        words.append(v[7 * m + 3 * t:])
+    return jnp.concatenate([*words, top[None]], axis=0)
+
+
+def opened(w, n):
+    m, t, rest = grouping(n)
+    top = w[w.shape[0] - 1]
+    values = []
+    if m:
+        even = top * (1 / EVEN)
+        first = [w[i * m:(i + 1) * m] for i in range(4)]
+        whole = [jnp.round(e * (1 / SLOT)) for e in first]
+        slot = [e - a * SLOT for e, a in zip(first, whole)]
+        low0 = jnp.round(slot[3] * (1 / (NINE * NINE)))
+        left = slot[3] - low0 * (NINE * NINE)
+        low1 = jnp.round(left * (1 / NINE))
+        low = [low0, low1, left - low1 * NINE]
+        whole += [h * STEP + e for h, e in zip(slot[:3], low)]
+        values += [a * even for a in whole]
+    if t:
+        fine, coarse = top * (1 / FINE), top * (1 / COARSE)
+        first, second = w[4 * m:4 * m + t], w[4 * m + t:4 * m + 2 * t]
+        a, b = jnp.round(first * (1 / SPLIT)), jnp.round(second * (1 / SPLIT))
+        c = (first - a * SPLIT) * BASE + (second - b * SPLIT)
+        values += [a * fine, b * fine, c * coarse]
+    if rest:
+        values.append(w[4 * m + 2 * t:4 * m + 2 * t + rest])
+    return jnp.concatenate(values, axis=0)
 
 
 def kernel(nz, rows, cols, stride, ta,
            b_ref, g_ref, out_ref,
-           bbuf, gt, cbuf, rc, s, ex1, ey1, ex2, ey2, rx1, ry1, rx2, ry2, own, z1r, z2s, z2r, f, ms, mr,
-           bsem, csem, x1sem, y1sem, x2sem, y2sem, z1sem, z2sem, msem):
+           bbuf, gbuf, gt, cbuf, rc, s, ex1, ey1, ex2, ey2, rx1, ry1, rx2, ry2, own, z1r, z2s, z2r, f, ms, mr,
+           bsem, gsem, csem, x1sem, y1sem, x2sem, y2sem, z1sem, z2sem, msem):
     c, o = lax.axis_index("chol"), lax.axis_index("orb")
     z, x = c // PAIR, lax.rem(c, PAIR)
     y, k = o // PAIR, lax.rem(o, PAIR)
@@ -133,6 +162,9 @@
     def far_copy(j):
         return remote(z2s.at[j, 1 - zh], z2r.at[j], z2sem.at[0, j], z2sem.at[1, j], far_id)
 
+    loads = [pltpu.make_async_copy(g_ref.at[q], gbuf.at[q], gsem.at[q]) for q in range(nvec)]
+    for copy in loads:
+        copy.start()
     for j in range(2):
         for side in range(2):
             for copy in fetches(j, side):
@@ -152,7 +184,7 @@
             greet((2 * o + h, c // 2))
 
     col = lax.broadcasted_iota(jnp.int32, (nocc, nocc), 1)
-    row = lax.broadcasted_iota(jnp.int32, (nocc, nocc), 0)
+    row = lax.broadcasted_iota(jnp.int32, (nocc, 1), 0)
     origin = row
     for xx in range(PAIR):
         for zz in range(nz):
@@ -160,7 +192,10 @@
             delta = (zz * PAIR + xx) * cols - start
             origin = jnp.where((row >= start) & (row < start + cols), row + delta, origin)
     pick = jnp.where(col == origin, 1.0, 0.0).astype(jnp.bfloat16)
-    parts = [jnp.dot(pick, g_ref[q], preferred_element_type=F32) for q in range(nvec)]
+    parts = []
+    for q in range(nvec):
+        loads[q].wait()
+        parts.append(jnp.dot(pick, gbuf[q], preferred_element_type=F32))
     gt[...] = jnp.concatenate(parts, axis=1).astype(jnp.bfloat16)
 
     count = 5 + jnp.where(c // 2 == o, 1, 2)
@@ -204,13 +239,13 @@
 
     def first_done(j):
         x1_copy(j).wait_recv()
-        arrived = opened(rx1[j], PAIR * ta % 3)
+        arrived = opened(rx1[j], PAIR * ta)
         s[j, 0, x, 0:ta] = s[j, 0, x, 0:ta] + arrived[0:ta]
         s[j, 1, x, 0:ta] = s[j, 1, x, 0:ta] + arrived[ta:2 * ta]
         ey2[j] = packed(s[j, 1 - y, x, 0:ta])
         y2_copy(j).start()
         y1_copy(j).wait_recv()
-        arrived = opened(ry1[j], PAIR * tb % 3)
+        arrived = opened(ry1[j], PAIR * tb)
         s[j, y, 0, ta:tiles] = s[j, y, 0, ta:tiles] + arrived[0:tb]
         s[j, y, 1, ta:tiles] = s[j, y, 1, ta:tiles] + arrived[tb:2 * tb]
         ex2[j] = packed(s[j, y, 1 - x, ta:tiles])
@@ -218,9 +253,9 @@
 
     def second_done(j):
         y2_copy(j).wait_recv()
-        own[j, 0:ta] = s[j, y, x, 0:ta] + opened(ry2[j], ta % 3)
+        own[j, 0:ta] = s[j, y, x, 0:ta] + opened(ry2[j], ta)
         x2_copy(j).wait_recv()
-        own[j, ta:tiles] = s[j, y, x, ta:tiles] + opened(rx2[j], tb % 3)
+        own[j, ta:tiles] = s[j, y, x, ta:tiles] + opened(rx2[j], tb)
         for h in range(2):
             near_copy(j, h).start()
 
@@ -305,7 +340,7 @@
     cols = nocc // (nz * PAIR)
     hx = nocc // PAIR
     tiles = hx // SUB
-    ta = (tiles + 1) // 2
+    ta = min(tiles, (tiles // 2 + 6) // 7 * 7)
     tb = tiles - ta
     tz = pl.cdiv(cols, SUB)
     nch = pl.cdiv(rows, LANES)
@@ -318,10 +353,11 @@
     return pl.pallas_call(
         functools.partial(kernel, nz, rows, cols, nmo // nocc, ta),
         out_shape=jax.ShapeDtypeStruct((rows, cols), F32),
-        in_specs=[pl.BlockSpec(memory_space=pl.ANY), pl.BlockSpec(memory_space=vmem)],
+        in_specs=[pl.BlockSpec(memory_space=pl.ANY), pl.BlockSpec(memory_space=pl.ANY)],
         out_specs=pl.BlockSpec(memory_space=vmem),
         scratch_shapes=[
             vmem((2 * PAIR, depth, PAIR * LANES), jnp.bfloat16),
+            vmem((nvec, nocc, rows), jnp.bfloat16),
             vmem((nocc, depth), jnp.bfloat16),
             vmem((nch, PAIR, PAIR, tiles, SUB, LANES), F32),
             vmem((nch, PAIR, PAIR, tiles, SUB, LANES), F32),
@@ -336,6 +372,7 @@
             vmem((2, tz * SUB, LANES), F32),
             vmem((2, tz * SUB, LANES), F32),
             dma((2 * PAIR, nvec * PAIR)),
+            dma((nvec,)),
             dma((2, nch)),
             dma((2, nch)),
             dma((2, nch)),

time: 61.5 us -> 63.1 us (1.026)
  Pallas kernels: 58.7 us -> 59.8 us
    pallas_call x1, Pallas kernels: 58.7 us -> 59.8 us  [mirrored_sums(): pl.pallas_call(functools.partial(kernel, nz, rows, cols, nmo // nocc, ta)...]
where the time goes in v2:
time: 63.1 us; the launch traced here: 61.9 us
  Pallas kernels  59.8 us (95%)
  local copies, waits for them, and re-layouts  2.19 us (3%)
    pallas_call x1, Pallas kernels, mirrored_sums(): pl.pallas_call(functools.partial(kernel, nz, rows, cols, nmo // nocc, ta)...  59.8 us
    pallas_call x1, local copies, waits for them, and re-layouts, mirrored_sums(): pl.pallas_call(functools.partial(kernel, nz, rows, cols, nmo // nocc, ta)...  2.19 us

profile of v2, /device:TPU:0, one launch (start us, length us, event | category | flops | bytes accessed | tf_op | source)
XLA Modules:
  0.0 61.9 jit_solution(2201499584267649118)
XLA Ops:
  0.0 59.8 %shard_map.28 = f32[1600,50]{1,0:T(8,128)} custom-call(bf16[2,1600,6400]{2,1,0:T(8,128)(2,1)} %b_ref.1, bf16[2,400,1600]{2,1,0:T(8,128)(2,1)} %bitcast.1), custom_call_target="tpu_custom_call" | custom-call | flops 16384000000 | bytes 40960000 | tf_op jit(solution)/shard_map/pallas_call | solution.py:353
  59.8 2.2 %copy.3 = f32[1600,50]{0,1:T(8,128)} copy(f32[1600,50]{1,0:T(8,128)} %shard_map.28) | data formatting | bytes 640000 | tf_op jit(solution)/shard_map/pallas_call | solution.py:353

commit v3 on v2

--- a/solution.py
+++ b/solution.py
@@ -10,7 +10,7 @@
 LANES = 128
 PAIR = 2
 SUB = 8
-LAGS = 1, 4, 7, 10, 13
+LAGS = 1, 3, 5, 7, 9
 MESH = pl.DeviceIdType.MESH
 F32 = jnp.float32
 

time: 63.1 us -> 61 us (0.967); the launches traced: 61.9 us -> 60.9 us
  Pallas kernels: 59.8 us -> 58.7 us
    pallas_call x1, Pallas kernels: 59.8 us -> 58.7 us  [mirrored_sums(): pl.pallas_call(functools.partial(kernel, nz, rows, cols, nmo // nocc, ta)...]
where the time goes in v3:
time: 61 us; the launch traced here: 60.9 us
  Pallas kernels  58.7 us (96%)
  local copies, waits for them, and re-layouts  2.19 us (4%)
    pallas_call x1, Pallas kernels, mirrored_sums(): pl.pallas_call(functools.partial(kernel, nz, rows, cols, nmo // nocc, ta)...  58.7 us
    pallas_call x1, local copies, waits for them, and re-layouts, mirrored_sums(): pl.pallas_call(functools.partial(kernel, nz, rows, cols, nmo // nocc, ta)...  2.19 us

profile of v3, /device:TPU:0, one launch (start us, length us, event | category | flops | bytes accessed | tf_op | source)
XLA Modules:
  0.0 60.9 jit_solution(2552417480256198186)
XLA Ops:
  0.0 58.7 %shard_map.28 = f32[1600,50]{1,0:T(8,128)} custom-call(bf16[2,1600,6400]{2,1,0:T(8,128)(2,1)} %b_ref.1, bf16[2,400,1600]{2,1,0:T(8,128)(2,1)} %bitcast.1), custom_call_target="tpu_custom_call" | custom-call | flops 16384000000 | bytes 40960000 | tf_op jit(solution)/shard_map/pallas_call | solution.py:353
  58.7 2.2 %copy.3 = f32[1600,50]{0,1:T(8,128)} copy(f32[1600,50]{1,0:T(8,128)} %shard_map.28) | data formatting | bytes 640000 | tf_op jit(solution)/shard_map/pallas_call | solution.py:353
